TPU v7x, 256 devices: a whole 4x4x8 slice. The times are simulated.
256 devices in a mesh: rep: 4 (over y), fsdp: 64 (over x, z, core).
Axes of the slice: x: 4, y: 4, z: 8, core: 2. Of those that a mesh axis runs over, the one named last changes fastest.
Arguments:
- activations: bfloat16 [65536, 512], P(('rep', 'fsdp')), may hold values from -6 to 6
- output_grads: bfloat16 [65536, 8192], P(('rep', 'fsdp'))
- master: float32 [8192, 512], P('fsdp'), may hold values from -6 to 6
- first_moment: float32 [8192, 512], P('fsdp'), may hold values from -4 to 4
- second_moment: float32 [8192, 512], P('fsdp'), may hold values from 0.2 to 2
Outputs:
- new_master: float32 [8192, 512], P('fsdp')
- new_first: float32 [8192, 512], P('fsdp')
- new_second: float32 [8192, 512], P('fsdp')
- params: bfloat16 [8192, 512], replicated
All inputs are finite; a program needn't handle non-finite values.
Results may differ from a plain program's by a relative error of at most 0.0004.
Values may be sent and summed in bfloat16 or wider, within the bound.
No kernel may reach another device: no remote copies, remote signals or barrier semaphores. Data moves between devices by JAX's collectives and lax.ppermute only.
A program may use at most 128 MiB of HBM per device.

v0:
```python
import jax
import jax.numpy as jnp
from jax import lax
from jax.sharding import PartitionSpec as P

dot_epsilon = 1e-06
beta_one = 0.9
beta_two = 0.95
adam_epsilon = 1e-08
learn_rate = 0.02
decay_rate = 0.1
contract_first = (((0,), (0,)), ((), ()))


def swapped(shard, axis, apart):
    return lax.ppermute(shard, axis, [(i, i ^ 1 << apart) for i in range(lax.axis_size(axis))])


def reversed_bits(number_in, bit_count):
    result = 0
    for position in range(bit_count):
        result = result << 1 | number_in >> position & 1
    return result


def local(activations, output_grads, master, first_moment, second_moment):
    grad_shard = lax.psum_scatter(
        lax.dot_general(
            output_grads, activations, contract_first, preferred_element_type=jnp.float32
        ),
        "fsdp",
        scatter_dimension=0,
        tiled=True,
    )
    replica_count = lax.axis_size("rep")
    level_total = replica_count.bit_length() - 1
    replica = lax.axis_index("rep")
    current = grad_shard
    for level_index in range(level_total):
        side_bit = replica >> level_index & 1
        low_side = side_bit == 0
        half_rows = current.shape[0] // 2
        lower_half = current[:half_rows]
        upper_half = current[half_rows:]
        kept_rows = jnp.where(low_side, lower_half, upper_half)
        outgoing = jnp.where(low_side, upper_half, lower_half)
        incoming = swapped(outgoing, "rep", level_index)
        left_vec = jnp.where(low_side, kept_rows, incoming)
        right_vec = jnp.where(low_side, incoming, kept_rows)
        partial_dots = jnp.stack(
            [
                jnp.sum(left_vec * right_vec),
                jnp.sum(left_vec * left_vec),
                jnp.sum(right_vec * right_vec),
            ]
        )
        totals = lax.psum(partial_dots, "fsdp")
        for inner_bit in range(level_index + 1):
            totals = totals + swapped(totals, "rep", inner_bit)
        left_coef = 1.0 - totals[0] / (2.0 * (totals[1] + dot_epsilon))
        right_coef = 1.0 - totals[0] / (2.0 * (totals[2] + dot_epsilon))
        current = left_coef * left_vec + right_coef * right_vec
    piece_rows = current.shape[0]
    gathered = lax.all_gather(current, "rep", axis=0, tiled=True)
    ordered = [
        gathered[
            reversed_bits(place, level_total)
            * piece_rows : (reversed_bits(place, level_total) + 1)
            * piece_rows
        ]
        for place in range(replica_count)
    ]
    combined = jnp.concatenate(ordered, axis=0)
    correct_one = 1.0 - (beta_one**50) ** 2
    correct_two = 1.0 - (beta_two**50) ** 2
    new_first = beta_one * first_moment + (1.0 - beta_one) * combined
    new_second = beta_two * second_moment + (1.0 - beta_two) * combined * combined
    update = (
        new_first / correct_one / (jnp.sqrt(new_second / correct_two) + adam_epsilon)
        + decay_rate * master
    )
    new_master = master - learn_rate * update
    params = lax.all_gather(new_master.astype(jnp.bfloat16), "fsdp", axis=0, tiled=True)
    return (new_master, new_first, new_second, params)


def solution(mesh):
    in_specs = (
        P(("rep", "fsdp"), None),
        P(("rep", "fsdp"), None),
        P("fsdp", None),
        P("fsdp", None),
        P("fsdp", None),
    )
    out_specs = (P("fsdp", None), P("fsdp", None), P("fsdp", None), P())
    return jax.shard_map(local, mesh=mesh, in_specs=in_specs, out_specs=out_specs, check_vma=False)
```

profile of v0, /device:TPU:1, one launch (start us, length us, event | category | flops | bytes accessed | tf_op | source)
XLA Modules:
  0.0 601.0 jit_solution(10944400333961210456)
XLA Ops:
  7.2 0.0 copy-start
  7.2 0.0 reduce-scatter.2.cloned.1.call-start
  7.2 0.9 copy-done
  8.1 10.3 %fusion.6 = f32[8192,512]{1,0:T(8,128)} fusion(bf16[256,8192]{1,0:T(8,128)(2,1)} %param.6, bf16[256,512]{1,0:T(8,128)(2,1)S(1)} %copy-done), kind=kOutput, calls=%fused_computation.27 | convolution fusion | flops 2147483648 | bytes 21233664 | tf_op jit(solution)/shard_map/dot_general | solution.py:28
  18.4 0.0 copy-start.1
  18.4 0.0 copy-start.2
  18.4 0.0 copy-start.3
  18.4 0.0 reduce-scatter.2.cloned.1.call-update
  18.4 0.0 all-gather.2.cloned.1.call-start
  18.5 189.2 %reduce-scatter.2.cloned.1.call-done = f32[128,512]{1,0:T(8,128)} async-done(((f32[8192,512]{1,0:T(8,128)}), f32[128,512]{1,0:T(8,128)}) %reduce-scatter.2.cloned.1.call-update) | async-done | bytes 262160 | tf_op jit(solution)/shard_map/reduce_scatter | solution.py:27
  207.7 1.0 slice_select_fusion
  208.7 0.9 collective-permute-start
  209.6 3.0 collective-permute-done
  212.6 1.6 multiply_reduce_fusion.2
  214.2 2.0 pad_maximum_fusion.1
  216.2 129.1 %psum.14 = f32[3]{0:T(128)S(1)} all-reduce(f32[3]{0:T(128)S(1)} %pad_maximum_fusion.1), channel_id=1, replica_groups=mesh['rep'=4,'fsdp'=64] {'fsdp'}, use_global_device_ids=true, to_apply=%region_4.5 | all-reduce | flops 3 | bytes 24 | tf_op jit(solution)/shard_map/psum | solution.py:57
  345.3 1.3 collective-permute-start.1
  346.6 1.2 collective-permute-done.1
  347.8 0.6 fusion.5
  351.0 2.6 collective-permute-start.2
  353.7 2.1 collective-permute-done.2
  355.7 0.6 multiply_reduce_fusion.5
  356.4 2.0 pad_maximum_fusion.2
  358.4 126.3 %psum.15 = f32[3]{0:T(128)S(1)} all-reduce(f32[3]{0:T(128)S(1)} %pad_maximum_fusion.2), channel_id=1, replica_groups=mesh['rep'=4,'fsdp'=64] {'fsdp'}, use_global_device_ids=true, to_apply=%region_8.9 | all-reduce | flops 3 | bytes 24 | tf_op jit(solution)/shard_map/psum | solution.py:57
  484.7 1.3 collective-permute-start.3
  486.0 1.2 collective-permute-done.3
  487.2 2.5 collective-permute-start.4
  489.7 1.3 collective-permute-done.4
  491.1 0.6 fusion.4
  494.3 9.5 %all_gather.6 = f32[128,512]{1,0:T(8,128)S(1)} all-gather(f32[32,512]{1,0:T(8,128)S(1)} %multiply_add_fusion.2), channel_id=1, replica_groups=mesh['rep'=4,'fsdp'=64] {'rep'}, dimensions={0}, use_global_device_ids=true | all-gather | bytes 327680 | tf_op jit(solution)/shard_map/all_gather | solution.py:64
  503.8 0.0 copy-done.1
  503.8 0.0 copy-done.2
  503.9 0.0 copy-done.3
  503.9 1.1 fusion.1
  504.9 0.0 all-gather.2.cloned.1.call-update
  504.9 81.9 %all-gather.2.cloned.1.call-done = bf16[8192,512]{1,0:T(8,128)(2,1)} async-done(((bf16[128,512]{1,0:T(8,128)(2,1)}), bf16[8192,512]{1,0:T(8,128)(2,1)}) %all-gather.2.cloned.1.call-update) | async-done | bytes 8388624 | tf_op jit(solution)/shard_map/all_gather | solution.py:83
  586.9 7.3 %copy.10 = bf16[8192,512]{1,0:T(8,128)(2,1)} copy(bf16[8192,512]{1,0:T(8,128)(2,1)} %all-gather.2.cloned.1.call-done) | data formatting | bytes 16777216
  (7 shorter events, 0.1 us)
Async XLA Ops:
  7.2 1.0 copy-start
  7.2 200.5 %reduce-scatter.2.cloned.1.call-start = ((), (), s32[]{:S(2)}) async-start(), calls=%async_computation.1 | async-start | bytes 17039360 | tf_op jit(solution)/shard_map/reduce_scatter | solution.py:27
  18.4 485.4 %copy-start.1 = (f32[128,512]{1,0:T(8,128)S(1)}, f32[128,512]{1,0:T(8,128)}, u32[]{:S(2)}) copy-start(f32[128,512]{1,0:T(8,128)} %param.7) | copy-start | bytes 786436
  18.4 485.4 %copy-start.2 = (f32[128,512]{1,0:T(8,128)S(1)}, f32[128,512]{1,0:T(8,128)}, u32[]{:S(2)}) copy-start(f32[128,512]{1,0:T(8,128)} %param.8) | copy-start | bytes 786436
  18.4 485.5 %copy-start.3 = (f32[128,512]{1,0:T(8,128)S(1)}, f32[128,512]{1,0:T(8,128)}, u32[]{:S(2)}) copy-start(f32[128,512]{1,0:T(8,128)} %param.9) | copy-start | bytes 786436
  18.4 568.4 %all-gather.2.cloned.1.call-start = ((), (), s32[]{:S(2)}) async-start(), calls=%async_computation.2 | async-start | bytes 8519680 | tf_op jit(solution)/shard_map/all_gather | solution.py:83
  208.7 3.9 collective-permute-start
  345.3 2.5 collective-permute-start.1
  351.0 4.7 collective-permute-start.2
  484.7 2.5 collective-permute-start.3
  487.2 3.9 collective-permute-start.4
Sparse Core Ops, SparseCore 0:
  18.6 189.1 reduce-scatter.1
  505.1 81.7 all-gather.1
where the time goes:
time: 601 us
  waiting for transfers between devices  280 us (47%)
  blocking collectives  265 us (44%)
  between operations  19.3 us (3%)
  matrix products  10.3 us (2%)
  local copies, waits for them, and re-layouts  9.44 us (2%)
  starting transfers between devices  8.68 us (1%)
  other arithmetic  8.38 us (1%)
    psum x2, blocking collectives, local(): totals = lax.psum(partial_dots, 'fsdp')  255 us
    reduce_scatter x1, waiting for transfers between devices, local(): lax.psum_scatter(lax.dot_general(output_grads, activations, contract_firs...  189 us
    all_gather x1, waiting for transfers between devices, local(): lax.all_gather(new_master.astype(jnp.bfloat16), 'fsdp', axis=0, tiled=True)  81.9 us
  transfers between devices with their start and end apart: 7, of which 7 were waited for; matrix products, arithmetic and copies ran while one was open for 0% of the time, Pallas kernels for 0%

commit v1 on v0

--- a/solution.py
+++ b/solution.py
@@ -10,6 +10,14 @@
 learn_rate = 0.02
 decay_rate = 0.1
 contract_first = (((0,), (0,)), ((), ()))
+
+
+def tiled_gather(array, axis, dim):
+    peers = lax.axis_size(axis)
+    repeats = [peers if d == dim else 1 for d in range(array.ndim)]
+    return lax.all_to_all(
+        jnp.tile(array, repeats), axis, split_axis=dim, concat_axis=dim, tiled=True
+    )
 
 
 def swapped(shard, axis, apart):
@@ -80,7 +88,7 @@
         + decay_rate * master
     )
     new_master = master - learn_rate * update
-    params = lax.all_gather(new_master.astype(jnp.bfloat16), "fsdp", axis=0, tiled=True)
+    params = tiled_gather(new_master.astype(jnp.bfloat16), "fsdp", 0)
     return (new_master, new_first, new_second, params)
 
 

time: 601 us -> 717 us (1.19)
  blocking collectives: 265 us -> 461 us
  waiting for transfers between devices: 280 us -> 198 us
    all_to_all x0 -> x1, blocking collectives: none -> 196 us  [tiled_gather(): lax.all_to_all(jnp.tile(array, repeats), axis, split_axis=dim, concat_axi...]
    all_gather x1 -> x0, waiting for transfers between devices: 81.9 us -> none  [local(): lax.all_gather(new_master.astype(jnp.bfloat16), 'fsdp', axis=0, tiled=True)]
  transfers between devices with their start and end apart: 7 -> 6, of which waited for: 7 -> 6; matrix products, arithmetic and copies ran while one was open for 0% -> 0% of each run, Pallas kernels for 0% -> 0%
where the time goes in v1:
time: 717 us; the launch traced here: 716 us
  blocking collectives  461 us (64%)
  waiting for transfers between devices  198 us (28%)
  between operations  19.3 us (3%)
  local copies, waits for them, and re-layouts  10.4 us (1%)
  matrix products  10.3 us (1%)
  starting transfers between devices  8.64 us (1%)
  other arithmetic  8.34 us (1%)
    psum x2, blocking collectives, local(): totals = lax.psum(partial_dots, 'fsdp')  255 us
    all_to_all x1, blocking collectives, tiled_gather(): lax.all_to_all(jnp.tile(array, repeats), axis, split_axis=dim, concat_axi...  196 us
    reduce_scatter x1, waiting for transfers between devices, local(): lax.psum_scatter(lax.dot_general(output_grads, activations, contract_firs...  189 us
  transfers between devices with their start and end apart: 6, of which 6 were waited for; matrix products, arithmetic and copies ran while one was open for 0% of the time, Pallas kernels for 0%

profile of v1, /device:TPU:1, one launch (start us, length us, event | category | flops | bytes accessed | tf_op | source)
XLA Modules:
  0.0 716.2 jit_solution(7639712770253166810)
XLA Ops:
  7.2 0.0 copy-start
  7.2 0.0 reduce-scatter.2.cloned.1.call-start
  7.2 0.9 copy-done
  8.1 10.3 %fusion.6 = f32[8192,512]{1,0:T(8,128)} fusion(bf16[256,8192]{1,0:T(8,128)(2,1)} %param.6, bf16[256,512]{1,0:T(8,128)(2,1)S(1)} %copy-done), kind=kOutput, calls=%fused_computation.27 | convolution fusion | flops 2147483648 | bytes 21233664 | tf_op jit(solution)/shard_map/dot_general | solution.py:36
  18.4 0.0 copy-start.1
  18.4 0.0 copy-start.2
  18.4 0.0 copy-start.3
  18.4 0.0 reduce-scatter.2.cloned.1.call-update
  18.4 189.3 %reduce-scatter.2.cloned.1.call-done = f32[128,512]{1,0:T(8,128)} async-done(((f32[8192,512]{1,0:T(8,128)}), f32[128,512]{1,0:T(8,128)}) %reduce-scatter.2.cloned.1.call-update) | async-done | bytes 262160 | tf_op jit(solution)/shard_map/reduce_scatter | solution.py:35
  207.7 1.0 slice_select_fusion
  208.7 0.9 collective-permute-start
  209.6 3.0 collective-permute-done
  212.6 1.6 multiply_reduce_fusion.2
  214.2 2.0 pad_maximum_fusion.1
  216.2 129.1 %psum.14 = f32[3]{0:T(128)S(1)} all-reduce(f32[3]{0:T(128)S(1)} %pad_maximum_fusion.1), channel_id=1, replica_groups=mesh['rep'=4,'fsdp'=64] {'fsdp'}, use_global_device_ids=true, to_apply=%region_4.5 | all-reduce | flops 3 | bytes 24 | tf_op jit(solution)/shard_map/psum | solution.py:65
  345.3 1.3 collective-permute-start.1
  346.6 1.2 collective-permute-done.1
  347.8 0.6 fusion.5
  351.0 2.6 collective-permute-start.2
  353.7 2.1 collective-permute-done.2
  355.7 0.6 multiply_reduce_fusion.5
  356.4 2.0 pad_maximum_fusion.2
  358.4 126.3 %psum.15 = f32[3]{0:T(128)S(1)} all-reduce(f32[3]{0:T(128)S(1)} %pad_maximum_fusion.2), channel_id=1, replica_groups=mesh['rep'=4,'fsdp'=64] {'fsdp'}, use_global_device_ids=true, to_apply=%region_8.9 | all-reduce | flops 3 | bytes 24 | tf_op jit(solution)/shard_map/psum | solution.py:65
  484.7 1.3 collective-permute-start.3
  486.0 1.2 collective-permute-done.3
  487.2 2.5 collective-permute-start.4
  489.7 1.3 collective-permute-done.4
  491.1 0.6 fusion.4
  494.3 9.5 %all_gather.3 = f32[128,512]{1,0:T(8,128)S(1)} all-gather(f32[32,512]{1,0:T(8,128)S(1)} %multiply_add_fusion.2), channel_id=1, replica_groups=mesh['rep'=4,'fsdp'=64] {'rep'}, dimensions={0}, use_global_device_ids=true | all-gather | bytes 327680 | tf_op jit(solution)/shard_map/all_gather | solution.py:72
  503.8 0.0 copy-done.1
  503.8 0.0 copy-done.2
  503.9 0.0 copy-done.3
  503.9 1.0 fusion.1
  504.9 1.0 tile.2
  505.9 196.2 %all_to_all.9 = bf16[64,128,512]{2,1,0:T(8,128)(2,1)} all-to-all(bf16[64,128,512]{2,1,0:T(8,128)(2,1)S(1)} %tile.2), channel_id=1, replica_groups=mesh['rep'=4,'fsdp'=64] {'fsdp'}, dimensions={0} | all-to-all | bytes 16777216 | tf_op jit(solution)/shard_map/all_to_all | solution.py:18
  702.1 7.3 %copy.10 = bf16[8192,512]{1,0:T(8,128)(2,1)} copy(bf16[8192,512]{1,0:T(8,128)(2,1)} %bitcast.13) | data formatting | bytes 16777216
  (7 shorter events, 0.1 us)
Async XLA Ops:
  7.2 1.0 copy-start
  7.2 200.5 %reduce-scatter.2.cloned.1.call-start = ((), (), s32[]{:S(2)}) async-start(), calls=%async_computation.2 | async-start | bytes 17039360 | tf_op jit(solution)/shard_map/reduce_scatter | solution.py:35
  18.4 485.4 %copy-start.1 = (f32[128,512]{1,0:T(8,128)S(1)}, f32[128,512]{1,0:T(8,128)}, u32[]{:S(2)}) copy-start(f32[128,512]{1,0:T(8,128)} %param.7) | copy-start | bytes 786436
  18.4 485.4 %copy-start.2 = (f32[128,512]{1,0:T(8,128)S(1)}, f32[128,512]{1,0:T(8,128)}, u32[]{:S(2)}) copy-start(f32[128,512]{1,0:T(8,128)} %param.8) | copy-start | bytes 786436
  18.4 485.5 %copy-start.3 = (f32[128,512]{1,0:T(8,128)S(1)}, f32[128,512]{1,0:T(8,128)}, u32[]{:S(2)}) copy-start(f32[128,512]{1,0:T(8,128)} %param.9) | copy-start | bytes 786436
  208.7 3.9 collective-permute-start
  345.3 2.5 collective-permute-start.1
  351.0 4.7 collective-permute-start.2
  484.7 2.5 collective-permute-start.3
  487.2 3.9 collective-permute-start.4
Sparse Core Ops, SparseCore 0:
  18.6 189.1 reduce-scatter.1
